TPU v7x, 512 devices: a whole 4x8x8 slice. The times are simulated.
512 devices in a mesh: video: 16 (over x, z_hi, core), tm: 32 (over y, z_lo).
Axes of the slice: x: 4, y: 8, z: 8 (z_hi: 2, z_lo: 4; z = z_hi * 4 + z_lo), core: 2. Of those that a mesh axis runs over, the one named last changes fastest.
Arguments:
- frames: bfloat16 [512, 28, 28, 704], P(('video', 'tm')), parts along dimension 0, may hold values from -6 to 6
- clip_cut: int32 [512], P(('video', 'tm')), parts along dimension 0, may hold values 0 or 1
- space_kernel: float32 [49, 704], replicated, may hold values from -0.8 to 0.8
- time_kernel: float32 [3, 704], replicated, may hold values from -3 to 3
- conv_bias: float32 [704], replicated, may hold values from -3 to 3
- norm_gain: float32 [704], replicated, may hold values from 0.5 to 1.5
- norm_bias: float32 [704], replicated, may hold values from -3 to 3
- up_weight: bfloat16 [704, 2816], P(None, 'tm'), may hold values from -0.21875 to 0.21875
- up_bias: float32 [2816], replicated, may hold values from -3 to 3
- grn_gamma: float32 [2816], replicated, may hold values from -3 to 3
- grn_beta: float32 [2816], replicated, may hold values from -3 to 3
- down_weight: bfloat16 [2816, 704], P('tm'), may hold values from -0.109375 to 0.109375
- down_bias: float32 [704], replicated, may hold values from -3 to 3
Outputs:
- block_out: bfloat16 [512, 28, 28, 704], P(('video', 'tm')), parts along dimension 0
There are 16 independent parts, one for each index of `video`. A program takes and returns all parts, laid end to end along the dimension named above; an argument that names none is the same for every part. Nothing has to cross between parts.
All inputs are finite; a program needn't handle non-finite values. No bound on the sum of `clip_cut` on one device may be relied on, other than what follows from the above.
Results may differ from a plain program's by a relative error of at most 0.0054.
Values may be sent and summed in bfloat16 or wider, within the bound.
No kernel may reach another device: no remote copies, remote signals or barrier semaphores. Data moves between devices by JAX's collectives and lax.ppermute only.
A program may use at most 64 MiB of HBM per device.

v0:
```python
import jax
import jax.numpy as jnp
from jax import lax
from jax.sharding import PartitionSpec as P


def from_behind(value, axis, by):
    count = lax.axis_size(axis)
    pairs = [(i, i + by) for i in range(count) if 0 <= i + by < count]
    return lax.ppermute(value, axis, pairs)


def space_time(frames, prev_side, next_side, space_kernel, time_kernel, conv_bias):
    padded = jnp.pad(frames, ((0, 0), (3, 3), (3, 3), (0, 0)))
    total = jnp.zeros(frames.shape, jnp.float32)
    for row_off in range(7):
        for col_off in range(7):
            window = padded[
                :, row_off : row_off + frames.shape[1], col_off : col_off + frames.shape[2], :
            ]
            total = total + window.astype(jnp.float32) * space_kernel[7 * row_off + col_off]
    total = total + time_kernel[0] * prev_side.astype(jnp.float32)
    total = total + time_kernel[1] * frames.astype(jnp.float32)
    total = total + time_kernel[2] * next_side.astype(jnp.float32)
    return total + conv_bias


def layer_norm(conv, norm_gain, norm_bias):
    mean_val = jnp.mean(conv, axis=-1, keepdims=True)
    centered = conv - mean_val
    var_val = jnp.mean(centered * centered, axis=-1, keepdims=True)
    return (centered / jnp.sqrt(var_val + 1e-06) * norm_gain + norm_bias).astype(jnp.bfloat16)


def response_norm(hidden, grn_gamma, grn_beta, frame_count):
    hid32 = hidden.astype(jnp.float32).reshape(frame_count, -1, hidden.shape[-1])
    energy = jnp.sqrt(jnp.sum(hid32 * hid32, axis=1, keepdims=True))
    ratio = energy / (jnp.mean(energy, axis=2, keepdims=True) + 1e-06)
    result = grn_gamma * hid32 * ratio + grn_beta + hid32
    return result.reshape(hidden.shape).astype(jnp.bfloat16)


def per_device(
    frames,
    clip_cut,
    space_kernel,
    time_kernel,
    conv_bias,
    norm_gain,
    norm_bias,
    up_weight,
    up_bias,
    grn_gamma,
    grn_beta,
    down_weight,
    down_bias,
):
    frame_count = frames.shape[0]
    keep = (1 - clip_cut).astype(jnp.bfloat16)[:, None, None, None]
    masked = frames * keep
    from_before = from_behind(frames, "tm", 1)
    from_after = from_behind(masked, "tm", -1)
    prev_side = jnp.concatenate([from_before, frames[:-1]], axis=0) * keep
    next_side = jnp.concatenate([masked[1:], from_after], axis=0)
    conv = space_time(frames, prev_side, next_side, space_kernel, time_kernel, conv_bias)
    rows = conv.reshape(-1, conv.shape[-1])
    normed = layer_norm(rows, norm_gain, norm_bias)
    residual = frames.reshape(rows.shape).astype(jnp.float32)
    hidden = jax.nn.gelu(
        jnp.dot(
            normed,
            lax.all_gather(up_weight, "tm", axis=1, tiled=True),
            preferred_element_type=jnp.float32,
        )
        + up_bias,
        approximate=False,
    ).astype(jnp.bfloat16)
    grn = response_norm(hidden, grn_gamma, grn_beta, frame_count)
    whole_down = lax.all_gather(down_weight, "tm", axis=0, tiled=True)
    projected = jnp.dot(grn, whole_down, preferred_element_type=jnp.float32)
    result = projected + down_bias + residual
    return result.astype(jnp.bfloat16).reshape(frames.shape)


def solution(mesh):
    return jax.shard_map(
        per_device,
        mesh=mesh,
        in_specs=(
            P(("video", "tm"), None, None, None),
            P(("video", "tm")),
            P(),
            P(),
            P(),
            P(),
            P(),
            P(None, "tm"),
            P(),
            P(),
            P(),
            P("tm", None),
            P(),
        ),
        out_specs=P(("video", "tm"), None, None, None),
        check_vma=False,
    )
```

profile of v0, /device:TPU:2, one launch (start us, length us, event | category | flops | bytes accessed | tf_op | source)
XLA Modules:
  0.0 385.6 jit_solution(17446686696309131363)
XLA Ops:
  6.5 0.7 all-gather.3.cloned.1.call-update
  7.3 0.0 all-gather.5.cloned.1.call-start
  8.0 2.5 broadcast_multiply_fusion
  10.5 1.4 collective-permute-start.1
  12.0 6.0 %collective-permute-start = (bf16[1,28,28,704]{3,2,1,0:T(8,128)(2,1)S(1)}, bf16[1,28,28,704]{3,2,1,0:T(8,128)(2,1)}, u32[]{:S(2)}, u32[]{:S(2)}) collective-permute-start(bf16[1,28,28,704]{3,2,1,0:T(8,128)(2,1)S(1)} %copy-done), channel_id=1, source_target_pairs={{0,1},{1,2},{2,3},{3,4},{4,5},{5,6},{6,7},{7,8},{8,9},{9,10},{10,1... | collective-permute-start | bytes 3311624 | tf_op jit(solution)/shard_map/ppermute | solution.py:10
  17.9 0.0 all-gather.5.cloned.1.call-update
  18.0 1.6 reshape.250
  19.6 0.1 slice_reduce_fusion.2
  19.7 0.2 slice_reduce_fusion.50
  19.9 0.2 slice_reduce_fusion.51
  20.1 29.9 %collective-permute-done.1 = bf16[1,28,28,704]{3,2,1,0:T(8,128)(2,1)S(1)} collective-permute-done((bf16[1,28,28,704]{3,2,1,0:T(8,128)(2,1)}, bf16[1,28,28,704]{3,2,1,0:T(8,128)(2,1)S(1)}, u32[]{:S(2)}, u32[]{:S(2)}) %collective-permute-start.1) | collective-permute-done | bytes 1103904 | tf_op jit(solution)/shard_map/ppermute | solution.py:10
  50.0 68.8 %collective-permute-done = bf16[1,28,28,704]{3,2,1,0:T(8,128)(2,1)} collective-permute-done((bf16[1,28,28,704]{3,2,1,0:T(8,128)(2,1)S(1)}, bf16[1,28,28,704]{3,2,1,0:T(8,128)(2,1)}, u32[]{:S(2)}, u32[]{:S(2)}) %collective-permute-start) | collective-permute-done | bytes 1103904 | tf_op jit(solution)/shard_map/ppermute | solution.py:10
  118.8 53.5 %fusion.25 = (f32[28,28]{1,0:T(8,128)S(1)}, f32[1,28,28,704]{3,2,1,0:T(8,128)S(1)}) fusion(f32[704]{0:T(1024)S(1)} %copy-done.5, bf16[1,28,28,704]{3,2,1,0:T(8,128)(2,1)} %copy-done.2, f32[704]{0:T(1024)S(1)} %get-tuple-element.55, f32[704]{0:T(1024)S(1)} %get-tuple-element.56, bf16[1,28,28,704]{3,2,1,0:T(8,128)(2,1)} %collective-permute-done, bf16[]{:T(256)} %bitcast, ...), kind=kLoop, calls=%fused_computation.143 | loop fusion | flops 87757040 | bytes 5671746 | tf_op jit(solution)/shard_map/reduce_sum | solution.py:29
  172.3 0.0 copy-start.9
  172.3 1.5 reshape.248
  173.9 0.1 div.33
  174.0 0.4 multiply_reduce_fusion
  174.4 0.1 sqrt.25
  174.6 25.7 %all-gather.3.cloned.1.call-done = bf16[704,2816]{0,1:T(8,128)(2,1)} async-done(((bf16[704,88]{0,1:T(8,128)(2,1)}), bf16[704,2816]{0,1:T(8,128)(2,1)}) %all-gather.3.cloned.1.call-update) | async-done | bytes 3964944 | tf_op jit(solution)/shard_map/all_gather | solution.py:72
  200.3 26.3 %fusion.5 = (f32[2816]{0:T(1024)S(1)}, bf16[784,2816]{1,0:T(8,128)(2,1)}) fusion(f32[2816]{0:T(1024)S(1)} %copy-done.6, bf16[704,2816]{0,1:T(8,128)(2,1)} %all-gather.3.cloned.1.call-done, f32[784,704]{1,0:T(8,128)} %reshape.248, f32[704]{0:T(1024)S(1)} %copy-done.9, f32[704]{0:T(1024)S(1)} %copy-done.10, f32[784]{0:T(1024)S(1)} %sqrt.25, f32[784]{0:T(1024)S(1)} %div.33), kind=kOutput, calls=%fused_computation.9 | convolution fusion | flops 3263594752 | bytes 10622592 | tf_op jit(solution)/shard_map/dot_general | solution.py:70
  226.6 0.6 sqrt_reduce_fusion
  227.9 139.0 %all-gather.5.cloned.1.call-done = bf16[2816,704]{1,0:T(8,128)(2,1)} async-done(((bf16[88,704]{1,0:T(8,128)(2,1)}), bf16[2816,704]{1,0:T(8,128)(2,1)}) %all-gather.5.cloned.1.call-update) | async-done | bytes 3964944 | tf_op jit(solution)/shard_map/all_gather | solution.py:79
  366.8 8.8 %add_convert_fusion = bf16[784,704]{1,0:T(8,128)(2,1)} fusion(f32[784,704]{1,0:T(8,128)S(1)} %copy-done.1, bf16[2816,704]{1,0:T(8,128)(2,1)} %all-gather.5.cloned.1.call-done, bf16[784,2816]{1,0:T(8,128)(2,1)} %get-tuple-element.60, f32[2816]{0:T(1024)S(1)} %copy-done.7, f32[2816]{0:T(1024)S(1)} %sqrt_divide_fusion, f32[2816]{0:T(1024)S(1)} %copy-done.8, ...), kind=kOutput, calls=%fused_computation.80 | convolution fusion | flops 3123405824 | bytes 11728640 | tf_op jit(solution)/shard_map/dot_general | solution.py:80
  375.6 3.2 reshape.249
  (27 shorter events, 0.1 us)
Async XLA Ops:
  6.5 5.4 %copy-start = (bf16[1,28,28,704]{3,2,1,0:T(8,128)(2,1)S(1)}, bf16[1,28,28,704]{3,2,1,0:T(8,128)(2,1)}, u32[]{:S(2)}) copy-start(bf16[1,28,28,704]{3,2,1,0:T(8,128)(2,1)} %param.13) | copy-start | bytes 3311620
  6.5 193.8 %all-gather.3.cloned.1.call-start = ((), (), s32[]{:S(2)}) async-start(), calls=%async_computation | async-start | bytes 4460544 | tf_op jit(solution)/shard_map/all_gather | solution.py:72
  7.3 359.6 %all-gather.5.cloned.1.call-start = ((), (), s32[]{:S(2)}) async-start(), calls=%async_computation.1 | async-start | bytes 4460544 | tf_op jit(solution)/shard_map/all_gather | solution.py:79
  8.0 11.6 %copy-start.3 = (f32[49,704]{1,0:T(8,128)S(1)}, f32[49,704]{1,0:T(8,128)}, u32[]{:S(2)}) copy-start(f32[49,704]{1,0:T(8,128)} %param.15) | copy-start | bytes 413956
  8.0 11.6 %copy-start.4 = (f32[3,704]{1,0:T(4,128)S(1)}, f32[3,704]{1,0:T(4,128)}, u32[]{:S(2)}) copy-start(f32[3,704]{1,0:T(4,128)} %param.16) | copy-start | bytes 25348
  10.5 108.3 %copy-start.5 = (f32[704]{0:T(1024)S(1)}, f32[704]{0:T(1024)}, u32[]{:S(2)}) copy-start(f32[704]{0:T(1024)} %param.17) | copy-start | bytes 8452
  10.5 39.5 %collective-permute-start.1 = (bf16[1,28,28,704]{3,2,1,0:T(8,128)(2,1)}, bf16[1,28,28,704]{3,2,1,0:T(8,128)(2,1)S(1)}, u32[]{:S(2)}, u32[]{:S(2)}) collective-permute-start(bf16[1,28,28,704]{3,2,1,0:T(8,128)(2,1)} %broadcast_multiply_fusion), channel_id=1, source_target_pairs={{1,0},{2,1},{3,2},{4,3},{5,4},{6,5},{7,6},{8,7},{9,8},{10,9},{11,1... | collective-permute-start | bytes 3311624 | tf_op jit(solution)/shard_map/ppermute | solution.py:10
  12.0 106.8 %collective-permute-start = (bf16[1,28,28,704]{3,2,1,0:T(8,128)(2,1)S(1)}, bf16[1,28,28,704]{3,2,1,0:T(8,128)(2,1)}, u32[]{:S(2)}, u32[]{:S(2)}) collective-permute-start(bf16[1,28,28,704]{3,2,1,0:T(8,128)(2,1)S(1)} %copy-done), channel_id=1, source_target_pairs={{0,1},{1,2},{2,3},{3,4},{4,5},{5,6},{6,7},{7,8},{8,9},{9,10},{10,1... | collective-permute-start | bytes 3311624 | tf_op jit(solution)/shard_map/ppermute | solution.py:10
  50.0 68.8 %copy-start.2 = (bf16[1,28,28,704]{3,2,1,0:T(8,128)(2,1)}, bf16[1,28,28,704]{3,2,1,0:T(8,128)(2,1)S(1)}, u32[]{:S(2)}) copy-start(bf16[1,28,28,704]{3,2,1,0:T(8,128)(2,1)S(1)} %collective-permute-done.1) | copy-start | bytes 3311620
  172.3 28.0 %copy-start.6 = (f32[2816]{0:T(1024)S(1)}, f32[2816]{0:T(1024)}, u32[]{:S(2)}) copy-start(f32[2816]{0:T(1024)} %param.21) | copy-start | bytes 33796
  172.3 28.0 %copy-start.9 = (f32[704]{0:T(1024)S(1)}, f32[704]{0:T(1024)}, u32[]{:S(2)}) copy-start(f32[704]{0:T(1024)} %param.19) | copy-start | bytes 8452
  172.3 28.0 %copy-start.10 = (f32[704]{0:T(1024)S(1)}, f32[704]{0:T(1024)}, u32[]{:S(2)}) copy-start(f32[704]{0:T(1024)} %param.18) | copy-start | bytes 8452
  174.5 192.3 %copy-start.1 = (f32[784,704]{1,0:T(8,128)S(1)}, f32[784,704]{1,0:T(8,128)}, u32[]{:S(2)}) copy-start(f32[784,704]{1,0:T(8,128)} %reshape.250) | copy-start | bytes 6623236
  174.5 192.3 %copy-start.7 = (f32[2816]{0:T(1024)S(1)}, f32[2816]{0:T(1024)}, u32[]{:S(2)}) copy-start(f32[2816]{0:T(1024)} %param.23) | copy-start | bytes 33796
  174.5 192.3 %copy-start.8 = (f32[2816]{0:T(1024)S(1)}, f32[2816]{0:T(1024)}, u32[]{:S(2)}) copy-start(f32[2816]{0:T(1024)} %param.22) | copy-start | bytes 33796
  174.6 192.3 %copy-start.11 = (f32[704]{0:T(1024)S(1)}, f32[704]{0:T(1024)}, u32[]{:S(2)}) copy-start(f32[704]{0:T(1024)} %param.25) | copy-start | bytes 8452
Sparse Core Ops, SparseCore 0:
  9.4 190.8 all-gather.2
  202.4 164.4 all-gather.4
where the time goes:
time: 386 us
  waiting for transfers between devices  264 us (68%)
  other arithmetic  57.1 us (15%)
  matrix products  35 us (9%)
  between operations  14.9 us (4%)
  starting transfers between devices  7.45 us (2%)
  local copies, waits for them, and re-layouts  7.02 us (2%)
    all_gather x1, waiting for transfers between devices, per_device(): whole_down = lax.all_gather(down_weight, 'tm', axis=0, tiled=True)  139 us
    ppermute x2, waiting for transfers between devices, from_behind(): return lax.ppermute(value, axis, pairs)  98.7 us
    reduce_sum x1, other arithmetic, layer_norm(): mean_val = jnp.mean(conv, axis=-1, keepdims=True)  53.5 us
    dot_general x1, matrix products, per_device(): jnp.dot(normed, lax.all_gather(up_weight, 'tm', axis=1, tiled=True), pref...  26.3 us
    all_gather x1, waiting for transfers between devices, per_device(): lax.all_gather(up_weight, 'tm', axis=1, tiled=True)  25.7 us
    dot_general x1, matrix products, per_device(): projected = jnp.dot(grn, whole_down, preferred_element_type=jnp.float32)  8.75 us
  transfers between devices with their start and end apart: 4, of which 4 were waited for; matrix products, arithmetic and copies ran while one was open for 23% of the time, Pallas kernels for 0%

commit v1 on v0

--- a/solution.py
+++ b/solution.py
@@ -1,7 +1,24 @@
+import functools
 import jax
 import jax.numpy as jnp
 from jax import lax
 from jax.sharding import PartitionSpec as P
+from jax.lax import all_to_all, axis_size
+
+
+def bench_raise(in_array, axis_id):
+    return jnp.concatenate(
+        all_to_all(
+            jnp.stack([in_array] * axis_size(axis_id), axis=0),
+            axis_name=axis_id,
+            split_axis=0,
+            concat_axis=0,
+        ),
+        axis=1,
+    )
+
+
+use_slot = functools.partial(bench_raise, axis_id="tm")
 
 
 def from_behind(value, axis, by):
@@ -67,12 +84,7 @@
     normed = layer_norm(rows, norm_gain, norm_bias)
     residual = frames.reshape(rows.shape).astype(jnp.float32)
     hidden = jax.nn.gelu(
-        jnp.dot(
-            normed,
-            lax.all_gather(up_weight, "tm", axis=1, tiled=True),
-            preferred_element_type=jnp.float32,
-        )
-        + up_bias,
+        jnp.dot(normed, use_slot(up_weight), preferred_element_type=jnp.float32) + up_bias,
         approximate=False,
     ).astype(jnp.bfloat16)
     grn = response_norm(hidden, grn_gamma, grn_beta, frame_count)

time: 386 us -> 318 us (0.82)
  the two profiles are of different devices: /device:TPU:2 before, /device:TPU:346 now
where the time goes in v1:
time: 318 us
  waiting for transfers between devices  212 us (67%)
  matrix products  34.5 us (11%)
  other arithmetic  30 us (9%)
  starting transfers between devices  16.4 us (5%)
  between operations  14.9 us (5%)
  local copies, waits for them, and re-layouts  10 us (3%)
    ppermute x2, waiting for transfers between devices, from_behind(): return lax.ppermute(value, axis, pairs)  184 us
    all_gather x1, waiting for transfers between devices, per_device(): whole_down = lax.all_gather(down_weight, 'tm', axis=0, tiled=True)  27.7 us
    reduce_sum x1, other arithmetic, layer_norm(): mean_val = jnp.mean(conv, axis=-1, keepdims=True)  27.3 us
    dot_general x1, matrix products, per_device(): jnp.dot(normed, use_slot(up_weight), preferred_element_type=jnp.float32)  25.9 us
    all_to_all x1, starting transfers between devices, bench_raise(): all_to_all(jnp.stack([in_array] * axis_size(axis_id), axis=0), axis_name=...  10.4 us
    dot_general x1, matrix products, per_device(): projected = jnp.dot(grn, whole_down, preferred_element_type=jnp.float32)  8.68 us
  transfers between devices with their start and end apart: 4, of which 3 were waited for; matrix products, arithmetic and copies ran while one was open for 19% of the time, Pallas kernels for 0%

profile of v1, /device:TPU:346, one launch (start us, length us, event | category | flops | bytes accessed | tf_op | source)
XLA Modules:
  0.0 318.0 jit_solution(907168852933908370)
XLA Ops:
  6.5 3.2 stack.2
  9.7 10.4 %all-to-all-start = ((bf16[32,704,88]{1,2,0:T(8,128)(2,1)}), bf16[32,704,88]{1,2,0:T(8,128)(2,1)}, u32[]{:S(2)}, u32[]{:S(2)}) async-start(bf16[32,704,88]{1,2,0:T(8,128)(2,1)} %stack.2), calls=%async_computation | async-start | bytes 8650752 | tf_op jit(solution)/shard_map/all_to_all | solution.py:11
  20.1 0.0 all-gather.2.cloned.1.call-start
  20.8 1.2 broadcast_multiply_fusion
  22.0 2.6 collective-permute-start.1
  24.6 3.4 %collective-permute-start = (bf16[1,28,28,704]{3,2,1,0:T(8,128)(2,1)S(1)}, bf16[1,28,28,704]{3,2,1,0:T(8,128)(2,1)}, u32[]{:S(2)}, u32[]{:S(2)}) collective-permute-start(bf16[1,28,28,704]{3,2,1,0:T(8,128)(2,1)S(1)} %copy-done), channel_id=1, source_target_pairs={{0,1},{1,2},{2,3},{3,4},{4,5},{5,6},{6,7},{7,8},{8,9},{9,10},{10,1... | collective-permute-start | bytes 3311624 | tf_op jit(solution)/shard_map/ppermute | solution.py:27
  28.0 0.0 all-gather.2.cloned.1.call-update
  28.0 1.6 reshape.273
  29.6 0.1 slice_reduce_fusion.2
  29.8 0.2 slice_reduce_fusion.50
  29.9 0.2 slice_reduce_fusion.51
  30.1 176.5 %collective-permute-done.1 = bf16[1,28,28,704]{3,2,1,0:T(8,128)(2,1)S(1)} collective-permute-done((bf16[1,28,28,704]{3,2,1,0:T(8,128)(2,1)}, bf16[1,28,28,704]{3,2,1,0:T(8,128)(2,1)S(1)}, u32[]{:S(2)}, u32[]{:S(2)}) %collective-permute-start.1) | collective-permute-done | bytes 1103904 | tf_op jit(solution)/shard_map/ppermute | solution.py:27
  206.6 8.0 %collective-permute-done = bf16[1,28,28,704]{3,2,1,0:T(8,128)(2,1)} collective-permute-done((bf16[1,28,28,704]{3,2,1,0:T(8,128)(2,1)S(1)}, bf16[1,28,28,704]{3,2,1,0:T(8,128)(2,1)}, u32[]{:S(2)}, u32[]{:S(2)}) %collective-permute-start) | collective-permute-done | bytes 1103904 | tf_op jit(solution)/shard_map/ppermute | solution.py:27
  214.5 27.3 %fusion.21 = (f32[28,28]{1,0:T(8,128)S(1)}, f32[1,28,28,704]{3,2,1,0:T(8,128)S(1)}) fusion(f32[704]{0:T(1024)S(1)} %copy-done.4, bf16[1,28,28,704]{3,2,1,0:T(8,128)(2,1)S(1)} %collective-permute-done.1, f32[704]{0:T(1024)S(1)} %get-tuple-element.55, f32[704]{0:T(1024)S(1)} %get-tuple-element.56, bf16[1,28,28,704]{3,2,1,0:T(8,128)(2,1)} %collective-permute-done, ...), kind=kLoop, calls=%fused_computation.139 | loop fusion | flops 87757040 | bytes 5671746 | tf_op jit(solution)/shard_map/reduce_sum | solution.py:46
  241.9 0.4 multiply_reduce_fusion
  242.3 0.2 copy-done.5
  242.5 0.0 copy-done.6
  242.5 0.5 add_convert_fusion
  243.0 1.4 convert_element_type.236
  244.4 25.9 %fusion.5 = (f32[2816]{0:T(1024)S(1)}, bf16[784,2816]{1,0:T(8,128)(2,1)}) fusion(f32[2816]{0:T(1024)S(1)} %copy-done.7, bf16[784,704]{1,0:T(8,128)(2,1)} %convert_element_type.236, bf16[704,2816]{0,1:T(8,128)(2,1)} %bitcast.2), kind=kOutput, calls=%fused_computation.9 | convolution fusion | flops 3260835072 | bytes 9506816 | tf_op jit(solution)/shard_map/dot_general | solution.py:87
  270.3 0.6 sqrt_reduce_fusion
  271.6 27.7 %all-gather.2.cloned.1.call-done = bf16[2816,704]{1,0:T(8,128)(2,1)} async-done(((bf16[88,704]{1,0:T(8,128)(2,1)}), bf16[2816,704]{1,0:T(8,128)(2,1)}) %all-gather.2.cloned.1.call-update) | async-done | bytes 3964944 | tf_op jit(solution)/shard_map/all_gather | solution.py:91
  299.3 8.7 %add_convert_fusion.1 = bf16[784,704]{1,0:T(8,128)(2,1)} fusion(f32[784,704]{1,0:T(8,128)S(1)} %copy-done.1, bf16[2816,704]{1,0:T(8,128)(2,1)} %all-gather.2.cloned.1.call-done, bf16[784,2816]{1,0:T(8,128)(2,1)} %get-tuple-element.60, f32[2816]{0:T(1024)S(1)} %copy-done.8, f32[2816]{0:T(1024)S(1)} %sqrt_divide_fusion, f32[2816]{0:T(1024)S(1)} %copy-done.9, ...), kind=kOutput, calls=%fused_computation.81 | convolution fusion | flops 3123405824 | bytes 11728640 | tf_op jit(solution)/shard_map/dot_general | solution.py:92
  308.0 3.2 reshape.272
  (24 shorter events, 0.1 us)
Async XLA Ops:
  9.7 11.1 %copy-start = (bf16[1,28,28,704]{3,2,1,0:T(8,128)(2,1)S(1)}, bf16[1,28,28,704]{3,2,1,0:T(8,128)(2,1)}, u32[]{:S(2)}) copy-start(bf16[1,28,28,704]{3,2,1,0:T(8,128)(2,1)} %param.13) | copy-start | bytes 3311620
  9.7 234.7 %all-to-all-start = ((bf16[32,704,88]{1,2,0:T(8,128)(2,1)}), bf16[32,704,88]{1,2,0:T(8,128)(2,1)}, u32[]{:S(2)}, u32[]{:S(2)}) async-start(bf16[32,704,88]{1,2,0:T(8,128)(2,1)} %stack.2), calls=%async_computation | async-start | bytes 8650752 | tf_op jit(solution)/shard_map/all_to_all | solution.py:11
  20.1 279.2 %all-gather.2.cloned.1.call-start = ((), (), s32[]{:S(2)}) async-start(), calls=%async_computation.1 | async-start | bytes 4460544 | tf_op jit(solution)/shard_map/all_gather | solution.py:91
  20.8 8.8 %copy-start.2 = (f32[49,704]{1,0:T(8,128)S(1)}, f32[49,704]{1,0:T(8,128)}, u32[]{:S(2)}) copy-start(f32[49,704]{1,0:T(8,128)} %param.15) | copy-start | bytes 413956
  20.8 8.8 %copy-start.3 = (f32[3,704]{1,0:T(4,128)S(1)}, f32[3,704]{1,0:T(4,128)}, u32[]{:S(2)}) copy-start(f32[3,704]{1,0:T(4,128)} %param.16) | copy-start | bytes 25348
  22.0 192.5 %copy-start.4 = (f32[704]{0:T(1024)S(1)}, f32[704]{0:T(1024)}, u32[]{:S(2)}) copy-start(f32[704]{0:T(1024)} %param.17) | copy-start | bytes 8452
  22.0 184.6 %collective-permute-start.1 = (bf16[1,28,28,704]{3,2,1,0:T(8,128)(2,1)}, bf16[1,28,28,704]{3,2,1,0:T(8,128)(2,1)S(1)}, u32[]{:S(2)}, u32[]{:S(2)}) collective-permute-start(bf16[1,28,28,704]{3,2,1,0:T(8,128)(2,1)} %broadcast_multiply_fusion), channel_id=1, source_target_pairs={{1,0},{2,1},{3,2},{4,3},{5,4},{6,5},{7,6},{8,7},{9,8},{10,9},{11,1... | collective-permute-start | bytes 3311624 | tf_op jit(solution)/shard_map/ppermute | solution.py:27
  24.6 189.9 %collective-permute-start = (bf16[1,28,28,704]{3,2,1,0:T(8,128)(2,1)S(1)}, bf16[1,28,28,704]{3,2,1,0:T(8,128)(2,1)}, u32[]{:S(2)}, u32[]{:S(2)}) collective-permute-start(bf16[1,28,28,704]{3,2,1,0:T(8,128)(2,1)S(1)} %copy-done), channel_id=1, source_target_pairs={{0,1},{1,2},{2,3},{3,4},{4,5},{5,6},{6,7},{7,8},{8,9},{9,10},{10,1... | collective-permute-start | bytes 3311624 | tf_op jit(solution)/shard_map/ppermute | solution.py:27
  241.8 0.7 copy-start.5
  241.8 0.7 copy-start.6
  242.5 1.9 copy-start.7
  244.4 54.9 %copy-start.1 = (f32[784,704]{1,0:T(8,128)S(1)}, f32[784,704]{1,0:T(8,128)}, u32[]{:S(2)}) copy-start(f32[784,704]{1,0:T(8,128)} %reshape.273) | copy-start | bytes 6623236
  244.4 54.9 %copy-start.8 = (f32[2816]{0:T(1024)S(1)}, f32[2816]{0:T(1024)}, u32[]{:S(2)}) copy-start(f32[2816]{0:T(1024)} %param.23) | copy-start | bytes 33796
  244.4 54.9 %copy-start.9 = (f32[2816]{0:T(1024)S(1)}, f32[2816]{0:T(1024)}, u32[]{:S(2)}) copy-start(f32[2816]{0:T(1024)} %param.22) | copy-start | bytes 33796
  244.4 54.9 %copy-start.10 = (f32[704]{0:T(1024)S(1)}, f32[704]{0:T(1024)}, u32[]{:S(2)}) copy-start(f32[704]{0:T(1024)} %param.25) | copy-start | bytes 8452
Sparse Core Ops, SparseCore 0:
  28.1 271.1 all-gather.1
